TPU v7x, 512 devices: a whole 4x8x8 slice. The times are simulated.
512 devices in a mesh: lon: 128 (over y, x_hi, z), lat: 4 (over x_lo, core).
Axes of the slice: x: 4 (x_hi: 2, x_lo: 2; x = x_hi * 2 + x_lo), y: 8, z: 8, core: 2. Of those that a mesh axis runs over, the one named last changes fastest.
Arguments:
- obs_rows: bfloat16 [128, 4, 1024, 64], P('lon', 'lat'), may hold values from -6 to 6
- obs_cells: int32 [128, 4, 1024], P('lon', 'lat'), may hold values from 0 to 63
- obs_counts: int32 [128, 4], P('lon', 'lat'), may hold values from 128 to 1024, as said below
- enc_weight: bfloat16 [64, 1024], replicated, may hold values from -0.75 to 0.75
- near_kernel_weight: bfloat16 [3, 3, 64, 1024], replicated, may hold values from -0.25 to 0.25
- far_kernel_weight: bfloat16 [3, 3, 64, 1024], replicated, may hold values from -0.25 to 0.25
- mix_weight: bfloat16 [1024, 1024], replicated, may hold values from -0.1875 to 0.1875
Outputs:
- state: bfloat16 [1024, 32, 1024], P('lon', 'lat')
Inputs may be any that keep to these rules, and one draw needn't show every extreme that they name: `obs_cells`: cell index i * 8 + j within the sector and band; slots at or past the count are ignored. `obs_counts`: live slots come first; some sector and band has all 1024 slots live.
All inputs are finite; a program needn't handle non-finite values.
Results may differ from a plain program's by a relative error of at most 0.006.
Values may be sent and summed in bfloat16 or wider, within the bound.
A program may use at most 128 MiB of HBM per device.

v0:
```python
import jax
import jax.numpy as jnp
from jax import lax
from jax.sharding import PartitionSpec as P

FAR_DILATION = 8
BAND_LAT_CELLS = 8
SECTOR_LON_CELLS = 8


def padded(array, sides, width, wrap):
    for axis, dim in sides:
        peers, length = (lax.axis_size(axis), array.shape[dim])
        up = [(i, (i + 1) % peers) for i in range(peers if wrap else peers - 1)]
        down = [(j, i) for i, j in up]
        last = lax.slice_in_dim(array, length - width, length, axis=dim)
        leading = lax.slice_in_dim(array, 0, width, axis=dim)
        before = lax.ppermute(last, axis, up)
        after = lax.ppermute(leading, axis, down)
        array = jnp.concatenate([before, array, after], axis=dim)
    return array


def passed_along(value, axis, steps):
    count = lax.axis_size(axis)
    pairs = [(source, (source + steps) % count) for source in range(count)]
    return lax.ppermute(value, axis, pairs)


def grouped_filter(extended, lon_starts, lat_starts, rows, cols, weight):
    channels = extended.shape[-1]
    width = weight.shape[2]
    groups = channels // width
    col_group = jnp.arange(channels, dtype=jnp.int32) // width
    same_group = col_group[:, None] == col_group[None, :]
    zero_value = jnp.zeros((), jnp.bfloat16)
    total = jnp.zeros((rows * cols, channels), jnp.float32)
    for first, lon_start in enumerate(lon_starts):
        for second, lat_start in enumerate(lat_starts):
            tiled = jnp.tile(weight[first, second], (groups, 1))
            dense = jnp.where(same_group, tiled, zero_value)
            piece = extended[lon_start : lon_start + rows, lat_start : lat_start + cols].reshape(
                rows * cols, channels
            )
            total = total + jnp.dot(piece, dense, preferred_element_type=jnp.float32)
    return total.reshape(rows, cols, channels)


def place_rows(rows_in, cells_in, count_in, enc_weight, first_row, kept_rows):
    channels = enc_weight.shape[1]
    encoded = jnp.dot(rows_in, enc_weight, preferred_element_type=jnp.float32).astype(jnp.bfloat16)
    live_slot = jnp.arange(rows_in.shape[0], dtype=jnp.int32) < count_in
    lat_cell = cells_in % BAND_LAT_CELLS
    lon_cell = cells_in // BAND_LAT_CELLS
    inside = live_slot & (lat_cell >= first_row) & (lat_cell < first_row + kept_rows)
    target = jnp.where(inside, lon_cell * kept_rows + lat_cell - first_row, -1)
    onehot = (
        jnp.arange(SECTOR_LON_CELLS * kept_rows, dtype=jnp.int32)[:, None] == target[None, :]
    ).astype(jnp.bfloat16)
    placed = jnp.dot(onehot, encoded, preferred_element_type=jnp.float32).astype(jnp.bfloat16)
    return placed.reshape(SECTOR_LON_CELLS, kept_rows, channels)


def on_device(
    obs_rows, obs_cells, obs_counts, enc_weight, near_kernel_weight, far_kernel_weight, mix_weight
):
    channels = mix_weight.shape[0]
    input_field = place_rows(
        obs_rows[0, 0], obs_cells[0, 0], obs_counts[0, 0], enc_weight, 0, BAND_LAT_CELLS
    )
    band_split = padded(input_field, (("lat", 1),), FAR_DILATION, False)
    neighbours = []
    for offset in (1, -1):
        neighbours.append(passed_along(band_split, "lon", offset))
    wide_field = jnp.concatenate([neighbours[0], band_split, neighbours[1]], 0)
    far_output = grouped_filter(
        wide_field,
        [0, SECTOR_LON_CELLS, 2 * SECTOR_LON_CELLS],
        [0, FAR_DILATION, 2 * FAR_DILATION],
        SECTOR_LON_CELLS,
        BAND_LAT_CELLS,
        far_kernel_weight,
    )
    rimmed = padded(input_field, (("lat", 1),), 1, False)
    rimmed = padded(rimmed, (("lon", 0),), 1, True)
    near_output = grouped_filter(
        rimmed, [0, 1, 2], [0, 1, 2], SECTOR_LON_CELLS, BAND_LAT_CELLS, near_kernel_weight
    )
    total = input_field.astype(jnp.float32) + near_output + far_output
    activ = jax.nn.gelu(total, approximate=True).astype(jnp.bfloat16)
    mixed = jnp.dot(
        activ.reshape(SECTOR_LON_CELLS * BAND_LAT_CELLS, channels),
        mix_weight,
        preferred_element_type=jnp.float32,
    )
    return (total + mixed.reshape(SECTOR_LON_CELLS, BAND_LAT_CELLS, channels)).astype(jnp.bfloat16)


def solution(mesh):
    return jax.shard_map(
        on_device,
        mesh=mesh,
        in_specs=(
            P("lon", "lat", None, None),
            P("lon", "lat", None),
            P("lon", "lat"),
            P(),
            P(),
            P(),
            P(),
        ),
        out_specs=P("lon", "lat", None),
        check_vma=False,
    )
```

profile of v0, /device:TPU:1, one launch (start us, length us, event | category | flops | bytes accessed | tf_op | source)
XLA Modules:
  0.0 80.6 jit_solution(13801278479025091219)
XLA Ops:
  0.8 0.8 fusion.66
  1.6 2.0 %fusion.26 = bf16[64,1024]{1,0:T(8,128)(2,1)S(1)} fusion(bf16[64,1024]{1,0:T(8,128)(2,1)} %param.10, bf16[1,1,1024,64]{2,3,1,0:T(8,128)(2,1)} %param.7, s32[1024]{0:T(1024)S(1)} %fusion.66), kind=kOutput, calls=%fused_computation.47 | convolution fusion | flops 269615104 | bytes 397312 | tf_op jit(solution)/shard_map/dot_general | solution.py:60
  3.6 4.5 %collective-permute-start.4 = (bf16[8,8,1024]{2,1,0:T(8,128)(2,1)S(1)}, bf16[8,8,1024]{2,1,0:T(8,128)(2,1)}, u32[]{:S(2)}, u32[]{:S(2)}) collective-permute-start(bf16[8,8,1024]{2,1,0:T(8,128)(2,1)S(1)} %bitcast.164), channel_id=1, source_target_pairs={{0,1},{1,2},{2,3},{4,5},{5,6},{6,7},{8,9},{9,10},{10,11},{12,13},{... | collective-permute-start | bytes 393224 | tf_op jit(solution)/shard_map/ppermute | solution.py:18
  8.1 6.2 %collective-permute-start.5 = (bf16[8,8,1024]{2,1,0:T(8,128)(2,1)S(1)}, bf16[8,8,1024]{2,1,0:T(8,128)(2,1)S(1)}, u32[]{:S(2)}, u32[]{:S(2)}) collective-permute-start(bf16[8,8,1024]{2,1,0:T(8,128)(2,1)S(1)} %bitcast.165), channel_id=1, source_target_pairs={{1,0},{2,1},{3,2},{5,4},{6,5},{7,6},{9,8},{10,9},{11,10},{13,12},{... | collective-permute-start | bytes 393224 | tf_op jit(solution)/shard_map/ppermute | solution.py:19
  14.3 0.7 fusion.82
  15.0 1.9 %collective-permute-start = (bf16[8,1,1024]{2,1,0:T(2,128)(2,1)}, bf16[8,1,1024]{2,1,0:T(2,128)(2,1)S(1)}, u32[]{:S(2)}, u32[]{:S(2)}) collective-permute-start(bf16[8,1,1024]{2,1,0:T(2,128)(2,1)} %get-tuple-element.27), channel_id=1, source_target_pairs={{0,1},{1,2},{2,3},{4,5},{5,6},{6,7},{8,9},{9,10},{10,11},{12,13},{... | collective-permute-start | bytes 49160 | tf_op jit(solution)/shard_map/ppermute | solution.py:18
  16.9 2.4 %collective-permute-start.1 = (bf16[8,1,1024]{2,1,0:T(2,128)(2,1)S(1)}, bf16[8,1,1024]{2,1,0:T(2,128)(2,1)S(1)}, u32[]{:S(2)}, u32[]{:S(2)}) collective-permute-start(bf16[8,1,1024]{2,1,0:T(2,128)(2,1)S(1)} %get-tuple-element.28), channel_id=1, source_target_pairs={{1,0},{2,1},{3,2},{5,4},{6,5},{7,6},{9,8},{10,9},{11,10},{13,12},{... | collective-permute-start | bytes 49160 | tf_op jit(solution)/shard_map/ppermute | solution.py:19
  19.3 2.7 %slice_bitcast_fusion.27 = (bf16[64,1024]{1,0:T(8,128)(2,1)}, bf16[64,1024]{1,0:T(8,128)(2,1)}, bf16[64,1024]{1,0:T(8,128)(2,1)}, bf16[64,1024]{1,0:T(8,128)(2,1...) fusion(bf16[3,3,64,1024]{3,2,1,0:T(8,128)(2,1)S(1)} %copy-done., ...), kind=kLoop, calls=%fused_computation.101 | loop fusion | bytes 4718592 | tf_op jit(solution)/shard_map/tile | solution.py:40
  22.1 10.0 %compare_select_fusion.8 = (bf16[16,64,1024]{2,1,0:T(8,128)(2,1)}, bf16[16,64,1024]{2,1,0:T(8,128)(2,1)S(1)}, bf16[16,64,1024]{2,1,0:T(8,128)(2,1)S(1)}, bf16[16...) fusion(s32[1024]{0:T(1024)S(1)} %add_select_fusion.1, ...), kind=kLoop, calls=%fused_computation.8 | loop fusion | flops 17825792 | bytes 35659776 | tf_op jit(solution)/shard_map/jit(_where)/select_n | solution.py:41
  32.4 0.8 %fusion = f32[64,1024]{1,0:T(8,128)S(1)} fusion(bf16[64,1024]{1,0:T(8,128)(2,1)S(1)} %fusion.26, bf16[1024,1024]{1,0:T(8,128)(2,1)S(1)} %bitcast.173, s32[1024]{0:T(1024)S(1)} %add_select_fusion.1), kind=kOutput, calls=%fused_computation.18 | convolution fusion | flops 136314880 | bytes 2494464 | tf_op jit(solution)/shard_map/dot_general | solution.py:45
  33.2 1.9 %collective-permute-start.2 = (bf16[1,10,1024]{2,1,0:T(8,128)(2,1)S(1)}, bf16[1,10,1024]{2,1,0:T(8,128)(2,1)S(1)}, u32[]{:S(2)}, u32[]{:S(2)}) collective-permute-start(bf16[1,10,1024]{2,1,0:T(8,128)(2,1)S(1)} %get-tuple-element.25), channel_id=1, source_target_pairs={{0,4},{4,8},{8,12},{12,16},{16,20},{20,24},{24,28},{28,32},{32,36}... | collective-permute-start | bytes 61448 | tf_op jit(solution)/shard_map/ppermute | solution.py:18
  35.2 12.7 %collective-permute-start.3 = (bf16[1,10,1024]{2,1,0:T(8,128)(2,1)S(1)}, bf16[1,10,1024]{2,1,0:T(8,128)(2,1)S(1)}, u32[]{:S(2)}, u32[]{:S(2)}) collective-permute-start(bf16[1,10,1024]{2,1,0:T(8,128)(2,1)S(1)} %get-tuple-element.26), channel_id=1, source_target_pairs={{4,0},{8,4},{12,8},{16,12},{20,16},{24,20},{28,24},{32,28},{36,32}... | collective-permute-start | bytes 61448 | tf_op jit(solution)/shard_map/ppermute | solution.py:19
  48.2 0.8 %fusion.1 = f32[64,1024]{1,0:T(8,128)S(1)} fusion(bf16[64,1024]{1,0:T(8,128)(2,1)S(1)} %fusion.26, bf16[1024,1024]{1,0:T(8,128)(2,1)S(1)} %bitcast.172, s32[1024]{0:T(1024)S(1)} %add_select_fusion.1), kind=kOutput, calls=%fused_computation.19 | convolution fusion | flops 136314880 | bytes 2494464 | tf_op jit(solution)/shard_map/dot_general | solution.py:45
  49.2 0.5 copy-done.10
  53.7 0.9 %copy-done.5 = bf16[16,64,1024]{2,1,0:T(8,128)(2,1)S(1)} copy-done((bf16[16,64,1024]{2,1,0:T(8,128)(2,1)S(1)}, bf16[16,64,1024]{2,1,0:T(8,128)(2,1)}, u32[]{:S(2)}) %copy-start.5) | copy-done | bytes 2097176
  56.0 1.1 %pad_maximum_fusion = bf16[8,24,1024]{2,1,0:T(8,128)(2,1)S(1)} fusion(bf16[8,8,1024]{2,1,0:T(8,128)(2,1)S(1)} %collective-permute-done.5, bf16[8,8,1024]{2,1,0:T(8,128)(2,1)S(1)} %bitcast.171, bf16[8,8,1024]{2,1,0:T(8,128)(2,1)} %collective-permute-done.4), kind=kLoop, calls=%fused_computation.50 | loop fusion | flops 1179648 | bytes 786432 | tf_op jit(solution)/shard_map/concatenate | solution.py:20
  57.1 1.9 %collective-permute-start.6 = (bf16[8,24,1024]{2,1,0:T(8,128)(2,1)S(1)}, bf16[8,24,1024]{2,1,0:T(8,128)(2,1)S(1)}, u32[]{:S(2)}, u32[]{:S(2)}) collective-permute-start(bf16[8,24,1024]{2,1,0:T(8,128)(2,1)S(1)} %pad_maximum_fusion), channel_id=1, source_target_pairs={{0,4},{4,8},{8,12},{12,16},{16,20},{20,24},{24,28},{28,32},{32,36}... | collective-permute-start | bytes 1179656 | tf_op jit(solution)/shard_map/ppermute | solution.py:27
  59.5 9.2 %collective-permute-start.7 = (bf16[8,24,1024]{2,1,0:T(8,128)(2,1)S(1)}, bf16[8,24,1024]{2,1,0:T(8,128)(2,1)S(1)}, u32[]{:S(2)}, u32[]{:S(2)}) collective-permute-start(bf16[8,24,1024]{2,1,0:T(8,128)(2,1)S(1)} %pad_maximum_fusion), channel_id=1, source_target_pairs={{0,508},{4,0},{8,4},{12,8},{16,12},{20,16},{24,20},{28,24},{32,28}... | collective-permute-start | bytes 1179656 | tf_op jit(solution)/shard_map/ppermute | solution.py:27
  68.7 1.4 %fusion.54 = f32[64,1024]{1,0:T(8,128)S(1)} fusion(bf16[1024,1024]{1,0:T(8,128)(2,1)S(1)} %bitcast.155, bf16[8,8,1024]{2,1,0:T(8,128)(2,1)} %collective-permute-done.4), kind=kOutput, calls=%fused_computation.92 | convolution fusion | flops 134217728 | bytes 2490368 | tf_op jit(solution)/shard_map/dot_general | solution.py:45
  70.1 4.4 %collective-permute-done.6 = bf16[8,24,1024]{2,1,0:T(8,128)(2,1)S(1)} collective-permute-done((bf16[8,24,1024]{2,1,0:T(8,128)(2,1)S(1)}, bf16[8,24,1024]{2,1,0:T(8,128)(2,1)S(1)}, u32[]{:S(2)}, u32[]{:S(2)}) %collective-permute-start.6) | collective-permute-done | bytes 393248 | tf_op jit(solution)/shard_map/ppermute | solution.py:27
  75.5 1.4 %collective-permute-done.7 = bf16[8,24,1024]{2,1,0:T(8,128)(2,1)S(1)} collective-permute-done((bf16[8,24,1024]{2,1,0:T(8,128)(2,1)S(1)}, bf16[8,24,1024]{2,1,0:T(8,128)(2,1)S(1)}, u32[]{:S(2)}, u32[]{:S(2)}) %collective-permute-start.7) | collective-permute-done | bytes 393248 | tf_op jit(solution)/shard_map/ppermute | solution.py:27
  78.4 0.5 fusion.21
  78.9 0.5 fusion.22
  79.4 1.1 %fusion.23 = bf16[8,8,1024]{2,1,0:T(8,128)(2,1)} fusion(bf16[1024,1024]{1,0:T(8,128)(2,1)S(1)} %copy-done, f32[64,1024]{1,0:T(8,128)S(1)} %fusion.22, f32[64,1024]{1,0:T(8,128)S(1)} %convolution_add_fusion.2, bf16[64,1024]{1,0:T(8,128)(2,1)S(1)} %fusion.26), kind=kOutput, calls=%fused_computation.46 | convolution fusion | flops 135331840 | bytes 2883584 | tf_op jit(solution)/shard_map/dot_general | solution.py:91
  (51 shorter events, 8.9 us)
Async XLA Ops:
  0.0 79.4 %copy-start = (bf16[1024,1024]{1,0:T(8,128)(2,1)S(1)}, bf16[1024,1024]{1,0:T(8,128)(2,1)}, u32[]{:S(2)}) copy-start(bf16[1024,1024]{1,0:T(8,128)(2,1)} %param.13) | copy-start | bytes 6291460
  0.0 19.3 %copy-start.11 = (bf16[3,3,64,1024]{3,2,1,0:T(8,128)(2,1)S(1)}, bf16[3,3,64,1024]{3,2,1,0:T(8,128)(2,1)}, u32[]{:S(2)}) copy-start(bf16[3,3,64,1024]{3,2,1,0:T(8,128)(2,1)} %param.12) | copy-start | bytes 3538948
  3.6 52.4 %collective-permute-start.4 = (bf16[8,8,1024]{2,1,0:T(8,128)(2,1)S(1)}, bf16[8,8,1024]{2,1,0:T(8,128)(2,1)}, u32[]{:S(2)}, u32[]{:S(2)}) collective-permute-start(bf16[8,8,1024]{2,1,0:T(8,128)(2,1)S(1)} %bitcast.164), channel_id=1, source_target_pairs={{0,1},{1,2},{2,3},{4,5},{5,6},{6,7},{8,9},{9,10},{10,11},{12,13},{... | collective-permute-start | bytes 393224 | tf_op jit(solution)/shard_map/ppermute | solution.py:18
  8.1 47.9 %collective-permute-start.5 = (bf16[8,8,1024]{2,1,0:T(8,128)(2,1)S(1)}, bf16[8,8,1024]{2,1,0:T(8,128)(2,1)S(1)}, u32[]{:S(2)}, u32[]{:S(2)}) collective-permute-start(bf16[8,8,1024]{2,1,0:T(8,128)(2,1)S(1)} %bitcast.165), channel_id=1, source_target_pairs={{1,0},{2,1},{3,2},{5,4},{6,5},{7,6},{9,8},{10,9},{11,10},{13,12},{... | collective-permute-start | bytes 393224 | tf_op jit(solution)/shard_map/ppermute | solution.py:19
  15.0 18.2 %collective-permute-start = (bf16[8,1,1024]{2,1,0:T(2,128)(2,1)}, bf16[8,1,1024]{2,1,0:T(2,128)(2,1)S(1)}, u32[]{:S(2)}, u32[]{:S(2)}) collective-permute-start(bf16[8,1,1024]{2,1,0:T(2,128)(2,1)} %get-tuple-element.27), channel_id=1, source_target_pairs={{0,1},{1,2},{2,3},{4,5},{5,6},{6,7},{8,9},{9,10},{10,11},{12,13},{... | collective-permute-start | bytes 49160 | tf_op jit(solution)/shard_map/ppermute | solution.py:18
  16.9 16.3 %collective-permute-start.1 = (bf16[8,1,1024]{2,1,0:T(2,128)(2,1)S(1)}, bf16[8,1,1024]{2,1,0:T(2,128)(2,1)S(1)}, u32[]{:S(2)}, u32[]{:S(2)}) collective-permute-start(bf16[8,1,1024]{2,1,0:T(2,128)(2,1)S(1)} %get-tuple-element.28), channel_id=1, source_target_pairs={{1,0},{2,1},{3,2},{5,4},{6,5},{7,6},{9,8},{10,9},{11,10},{13,12},{... | collective-permute-start | bytes 49160 | tf_op jit(solution)/shard_map/ppermute | solution.py:19
  22.1 10.0 %copy-start.13 = (bf16[64,1024]{1,0:T(8,128)(2,1)S(1)}, bf16[64,1024]{1,0:T(8,128)(2,1)}, u32[]{:S(2)}) copy-start(bf16[64,1024]{1,0:T(8,128)(2,1)} %get-tuple-element.50) | copy-start | bytes 393220
  32.4 15.5 %copy-start.12 = (bf16[64,1024]{1,0:T(8,128)(2,1)S(1)}, bf16[64,1024]{1,0:T(8,128)(2,1)}, u32[]{:S(2)}) copy-start(bf16[64,1024]{1,0:T(8,128)(2,1)} %get-tuple-element.16) | copy-start | bytes 393220
  33.2 15.8 %collective-permute-start.2 = (bf16[1,10,1024]{2,1,0:T(8,128)(2,1)S(1)}, bf16[1,10,1024]{2,1,0:T(8,128)(2,1)S(1)}, u32[]{:S(2)}, u32[]{:S(2)}) collective-permute-start(bf16[1,10,1024]{2,1,0:T(8,128)(2,1)S(1)} %get-tuple-element.25), channel_id=1, source_target_pairs={{0,4},{4,8},{8,12},{12,16},{16,20},{20,24},{24,28},{28,32},{32,36}... | collective-permute-start | bytes 61448 | tf_op jit(solution)/shard_map/ppermute | solution.py:18
  35.2 13.8 %collective-permute-start.3 = (bf16[1,10,1024]{2,1,0:T(8,128)(2,1)S(1)}, bf16[1,10,1024]{2,1,0:T(8,128)(2,1)S(1)}, u32[]{:S(2)}, u32[]{:S(2)}) collective-permute-start(bf16[1,10,1024]{2,1,0:T(8,128)(2,1)S(1)} %get-tuple-element.26), channel_id=1, source_target_pairs={{4,0},{8,4},{12,8},{16,12},{20,16},{24,20},{28,24},{32,28},{36,32}... | collective-permute-start | bytes 61448 | tf_op jit(solution)/shard_map/ppermute | solution.py:19
  48.2 1.6 %copy-start.10 = (bf16[16,64,1024]{2,1,0:T(8,128)(2,1)S(1)}, bf16[16,64,1024]{2,1,0:T(8,128)(2,1)}, u32[]{:S(2)}) copy-start(bf16[16,64,1024]{2,1,0:T(8,128)(2,1)} %get-tuple-element.42) | copy-start | bytes 6291460
  49.0 1.7 %copy-start.9 = (bf16[16,64,1024]{2,1,0:T(8,128)(2,1)S(1)}, bf16[16,64,1024]{2,1,0:T(8,128)(2,1)}, u32[]{:S(2)}) copy-start(bf16[16,64,1024]{2,1,0:T(8,128)(2,1)} %get-tuple-element.44) | copy-start | bytes 6291460
  49.8 1.7 %copy-start.8 = (bf16[16,64,1024]{2,1,0:T(8,128)(2,1)S(1)}, bf16[16,64,1024]{2,1,0:T(8,128)(2,1)}, u32[]{:S(2)}) copy-start(bf16[16,64,1024]{2,1,0:T(8,128)(2,1)} %get-tuple-element.41) | copy-start | bytes 6291460
  50.7 1.7 %copy-start.7 = (bf16[16,64,1024]{2,1,0:T(8,128)(2,1)S(1)}, bf16[16,64,1024]{2,1,0:T(8,128)(2,1)}, u32[]{:S(2)}) copy-start(bf16[16,64,1024]{2,1,0:T(8,128)(2,1)} %get-tuple-element.38) | copy-start | bytes 6291460
  51.5 1.7 %copy-start.6 = (bf16[16,64,1024]{2,1,0:T(8,128)(2,1)S(1)}, bf16[16,64,1024]{2,1,0:T(8,128)(2,1)}, u32[]{:S(2)}) copy-start(bf16[16,64,1024]{2,1,0:T(8,128)(2,1)} %get-tuple-element.40) | copy-start | bytes 6291460
  53.0 1.7 %copy-start.5 = (bf16[16,64,1024]{2,1,0:T(8,128)(2,1)S(1)}, bf16[16,64,1024]{2,1,0:T(8,128)(2,1)}, u32[]{:S(2)}) copy-start(bf16[16,64,1024]{2,1,0:T(8,128)(2,1)} %get-tuple-element.39) | copy-start | bytes 6291460
  53.7 1.7 %copy-start.4 = (bf16[16,64,1024]{2,1,0:T(8,128)(2,1)S(1)}, bf16[16,64,1024]{2,1,0:T(8,128)(2,1)}, u32[]{:S(2)}) copy-start(bf16[16,64,1024]{2,1,0:T(8,128)(2,1)} %get-tuple-element.37) | copy-start | bytes 6291460
  55.1 3.9 %copy-start.3 = (bf16[16,64,1024]{2,1,0:T(8,128)(2,1)S(1)}, bf16[16,64,1024]{2,1,0:T(8,128)(2,1)}, u32[]{:S(2)}) copy-start(bf16[16,64,1024]{2,1,0:T(8,128)(2,1)} %get-tuple-element.29) | copy-start | bytes 6291460
  56.0 12.8 %copy-start.2 = (bf16[16,64,1024]{2,1,0:T(8,128)(2,1)S(1)}, bf16[16,64,1024]{2,1,0:T(8,128)(2,1)}, u32[]{:S(2)}) copy-start(bf16[16,64,1024]{2,1,0:T(8,128)(2,1)} %get-tuple-element.33) | copy-start | bytes 6291460
  57.1 17.4 %collective-permute-start.6 = (bf16[8,24,1024]{2,1,0:T(8,128)(2,1)S(1)}, bf16[8,24,1024]{2,1,0:T(8,128)(2,1)S(1)}, u32[]{:S(2)}, u32[]{:S(2)}) collective-permute-start(bf16[8,24,1024]{2,1,0:T(8,128)(2,1)S(1)} %pad_maximum_fusion), channel_id=1, source_target_pairs={{0,4},{4,8},{8,12},{12,16},{16,20},{20,24},{24,28},{28,32},{32,36}... | collective-permute-start | bytes 1179656 | tf_op jit(solution)/shard_map/ppermute | solution.py:27
  59.0 15.5 %copy-start.1 = (bf16[16,64,1024]{2,1,0:T(8,128)(2,1)S(1)}, bf16[16,64,1024]{2,1,0:T(8,128)(2,1)}, u32[]{:S(2)}) copy-start(bf16[16,64,1024]{2,1,0:T(8,128)(2,1)} %get-tuple-element.34) | copy-start | bytes 6291460
  59.5 17.4 %collective-permute-start.7 = (bf16[8,24,1024]{2,1,0:T(8,128)(2,1)S(1)}, bf16[8,24,1024]{2,1,0:T(8,128)(2,1)S(1)}, u32[]{:S(2)}, u32[]{:S(2)}) collective-permute-start(bf16[8,24,1024]{2,1,0:T(8,128)(2,1)S(1)} %pad_maximum_fusion), channel_id=1, source_target_pairs={{0,508},{4,0},{8,4},{12,8},{16,12},{20,16},{24,20},{28,24},{32,28}... | collective-permute-start | bytes 1179656 | tf_op jit(solution)/shard_map/ppermute | solution.py:27
where the time goes:
time: 81 us; the launch traced here: 80.6 us
  starting transfers between devices  40.8 us (50%)
  matrix products  13.4 us (17%)
  other arithmetic  12.1 us (15%)
  local copies, waits for them, and re-layouts  7.26 us (9%)
  waiting for transfers between devices  5.81 us (7%)
  between operations  1.23 us (2%)
    ppermute x3, starting transfers between devices, padded(): after = lax.ppermute(leading, axis, down)  21.3 us
    ppermute x2, starting transfers between devices, passed_along(): return lax.ppermute(value, axis, pairs)  11.1 us
    dot_general x18, matrix products, grouped_filter(): total = total + jnp.dot(piece, dense, preferred_element_type=jnp.float32)  10.2 us
    select_n x1, other arithmetic, grouped_filter(): dense = jnp.where(same_group, tiled, zero_value)  10 us
    ppermute x3, starting transfers between devices, padded(): before = lax.ppermute(last, axis, up)  8.32 us
    ppermute x2, waiting for transfers between devices, passed_along(): return lax.ppermute(value, axis, pairs)  5.79 us
    unnamed x28, local copies, waits for them, and re-layouts  3.36 us
    another operation x3, local copies, waits for them, and re-layouts, grouped_filter(): tiled = jnp.tile(weight[first, second], (groups, 1))  3.24 us
  transfers between devices with their start and end apart: 8, of which 2 were waited for; matrix products, arithmetic and copies ran while one was open for 27% of the time, Pallas kernels for 0%

commit v1 on v0

v1 whole, which is shorter than its diff:
```python
import functools

import jax
import jax.numpy as jnp
from jax import lax
from jax.experimental import pallas as pl
from jax.experimental.pallas import tpu as pltpu
from jax.sharding import PartitionSpec as P

LON = 8
LAT = 8
CELLS = LON * LAT
MESH = pl.DeviceIdType.MESH
OFFSETS = [(a, b) for a in (-1, 0, 1) for b in (-1, 0, 1)]
CENTRE = 4
CHUNK = 256


def slot_of(a, b):
    return (a + 1) * 3 + (b + 1)


def composite(enc, weight_ref, composite_ref, base, low_mask, high_mask):
    features, channels = enc.shape
    zero = jnp.zeros((features, 128), jnp.bfloat16)

    def tap(t, carry):
        taps = weight_ref[t // 3, t % 3]
        for start in range(0, channels, CHUNK):
            left = taps[:, start : start + 128]
            right = taps[:, start + 128 : start + 256]
            blocks = jnp.concatenate(
                [
                    jnp.concatenate([left * low_mask, zero], axis=1),
                    jnp.concatenate([left * high_mask, zero], axis=1),
                    jnp.concatenate([zero, right * low_mask], axis=1),
                    jnp.concatenate([zero, right * high_mask], axis=1),
                ],
                axis=0,
            )
            product = jnp.dot(
                enc[:, start : start + CHUNK], blocks, preferred_element_type=jnp.float32
            )
            row = pl.multiple_of((base + t) * features, features)
            composite_ref[pl.ds(row, features), start : start + CHUNK] = product.astype(
                jnp.bfloat16
            )
        return carry

    lax.fori_loop(0, 9, tap, 0)


def kernel(
    lon_count,
    lat_count,
    obs_hbm,
    cells_hbm,
    count_hbm,
    enc_hbm,
    near_hbm,
    far_hbm,
    mix_hbm,
    out_ref,
    obs_ref,
    cells_ref,
    count_ref,
    enc_ref,
    near_ref,
    far_ref,
    mix_ref,
    slots,
    composite_ref,
    total_ref,
    activ_ref,
    local_sems,
    send_sems,
    recv_sems,
):
    pairs = [
        (obs_hbm, obs_ref),
        (cells_hbm, cells_ref),
        (count_hbm, count_ref),
        (enc_hbm, enc_ref),
        (near_hbm, near_ref),
        (far_hbm, far_ref),
        (mix_hbm, mix_ref),
    ]
    loads = [
        pltpu.make_async_copy(source, target, local_sems.at[i])
        for i, (source, target) in enumerate(pairs)
    ]
    for load in loads:
        load.start()

    lon = lax.axis_index("lon")
    lat = lax.axis_index("lat")

    def peer(a, b):
        return {"lon": lax.rem(lon + a + lon_count, lon_count), "lat": lat + b}

    def with_peer(b, body):
        if b == 0:
            body()
        elif b < 0:
            pl.when(lat > 0)(body)
        else:
            pl.when(lat < lat_count - 1)(body)

    remote = [(a, b) for a, b in OFFSETS if (a, b) != (0, 0)]
    barrier = pltpu.get_barrier_semaphore()
    for a, b in remote:
        with_peer(
            b,
            lambda a=a, b=b: pl.semaphore_signal(
                barrier, inc=1, device_id=peer(a, b), device_id_type=MESH
            ),
        )

    for edge, b in ((0, -1), (lat_count - 1, 1)):

        @pl.when(lat == edge)
        def _(b=b):
            for a in (-1, 0, 1):
                slots[slot_of(a, b)] = jnp.zeros((CELLS, 128), jnp.bfloat16)

    loads[0].wait()
    loads[1].wait()
    loads[2].wait()
    cells = cells_ref[0]
    live = lax.broadcasted_iota(jnp.int32, cells.shape, 1) < count_ref[...]
    target = jnp.where(live, cells, -1)
    onehot = jnp.where(
        lax.broadcasted_iota(jnp.int32, (CELLS, cells.shape[1]), 0) == target, 1.0, 0.0
    ).astype(jnp.bfloat16)
    summed = lax.dot_general(
        onehot, obs_ref[0, 0], (((1,), (1,)), ((), ())), preferred_element_type=jnp.float32
    )
    high = summed.astype(jnp.bfloat16)
    low = (summed - high.astype(jnp.float32)).astype(jnp.bfloat16)
    slots[CENTRE] = jnp.concatenate([high, low], axis=1)

    lanes = lax.broadcasted_iota(jnp.int32, (64, 128), 1)
    low_mask = jnp.where(lanes < 64, 1.0, 0.0).astype(jnp.bfloat16)
    high_mask = jnp.where(lanes < 64, 0.0, 1.0).astype(jnp.bfloat16)

    loads[3].wait()
    loads[4].wait()
    enc = enc_ref[...]
    composite(enc, near_ref, composite_ref, 9, low_mask, high_mask)

    pl.semaphore_wait(barrier, jnp.where((lat == 0) | (lat == lat_count - 1), 5, 8))
    copies = []
    for a, b in remote:
        copies.append(
            (
                b,
                pltpu.make_async_remote_copy(
                    src_ref=slots.at[CENTRE],
                    dst_ref=slots.at[slot_of(-a, -b)],
                    send_sem=send_sems.at[slot_of(a, b)],
                    recv_sem=recv_sems.at[slot_of(-a, -b)],
                    device_id=peer(a, b),
                    device_id_type=MESH,
                ),
            )
        )
    for b, copy in copies:
        with_peer(b, copy.start)

    loads[5].wait()
    composite(enc, far_ref, composite_ref, 0, low_mask, high_mask)
    centre = slice(CENTRE * 64, CENTRE * 64 + 64)
    composite_ref[centre] = (
        composite_ref[centre].astype(jnp.float32) + enc.astype(jnp.float32)
    ).astype(jnp.bfloat16)

    for a, b in remote:
        arrival = pltpu.make_async_remote_copy(
            src_ref=slots.at[CENTRE],
            dst_ref=slots.at[slot_of(a, b)],
            send_sem=send_sems.at[slot_of(a, b)],
            recv_sem=recv_sems.at[slot_of(a, b)],
            device_id=peer(a, b),
            device_id_type=MESH,
        )
        with_peer(b, arrival.wait_recv)

    whole = [slots[i].astype(jnp.float32).reshape(LON, LAT, 128) for i in range(9)]
    lon_extended = [
        jnp.concatenate(
            [whole[slot_of(-1, b)][LON - 1 :], whole[slot_of(0, b)], whole[slot_of(1, b)][:1]], 0
        )
        for b in (-1, 0, 1)
    ]
    row = lax.broadcasted_iota(jnp.int32, (LON + 2, LAT, 128), 1)
    before = jnp.where(
        row == 0, pltpu.roll(lon_extended[0], 1, 1), pltpu.roll(lon_extended[1], 1, 1)
    )
    after = jnp.where(
        row == LAT - 1,
        pltpu.roll(lon_extended[2], LAT - 1, 1),
        pltpu.roll(lon_extended[1], LAT - 1, 1),
    )
    shifted = [before, lon_extended[1], after]
    taps = [piece.reshape(CELLS, 128) for piece in whole]
    for a in range(3):
        for b in range(3):
            taps.append(shifted[b][a : a + LON].reshape(CELLS, 128))
    left_half = lax.broadcasted_iota(jnp.int32, (CELLS, 128), 1) < 64
    columns = []
    for i in range(0, 18, 2):
        first, second = taps[i], taps[i + 1]
        highs = jnp.where(left_half, first, pltpu.roll(second, 64, 1))
        lows = jnp.where(left_half, pltpu.roll(first, 64, 1), second)
        columns.append(jnp.concatenate([highs, lows], axis=0).astype(jnp.bfloat16))
    lhs = jnp.concatenate(columns, axis=1)

    channels = enc.shape[1]
    for start in range(0, channels, CHUNK):
        block = slice(start, start + CHUNK)
        product = jnp.dot(lhs, composite_ref[:, block], preferred_element_type=jnp.float32)
        total = product[:CELLS] + product[CELLS:]
        total_ref[:, block] = total
        inner = 0.7978845608 * (total + 0.044715 * (total * total * total))
        activ_ref[:, block] = (0.5 * total * (1.0 + jnp.tanh(inner))).astype(jnp.bfloat16)

    loads[6].wait()
    activ = activ_ref[...]
    for start in range(0, channels, CHUNK):
        block = slice(start, start + CHUNK)
        mixed = jnp.dot(activ, mix_ref[:, block], preferred_element_type=jnp.float32)
        out_ref[:, :, block] = (
            (total_ref[:, block] + mixed).astype(jnp.bfloat16).reshape(LON, LAT, CHUNK)
        )

    for b, copy in copies:
        with_peer(b, copy.wait_send)


def on_device(
    lon_count,
    lat_count,
    obs_rows,
    obs_cells,
    obs_counts,
    enc_weight,
    near_kernel_weight,
    far_kernel_weight,
    mix_weight,
):
    channels = mix_weight.shape[0]
    operands = (
        jnp.swapaxes(obs_rows, 2, 3),
        obs_cells,
        obs_counts,
        enc_weight,
        near_kernel_weight,
        far_kernel_weight,
        mix_weight,
    )
    return pl.pallas_call(
        functools.partial(kernel, lon_count, lat_count),
        out_shape=jax.ShapeDtypeStruct((LON, LAT, channels), jnp.bfloat16),
        in_specs=[pl.BlockSpec(memory_space=pltpu.HBM)] * len(operands),
        out_specs=pl.BlockSpec(memory_space=pltpu.VMEM),
        scratch_shapes=[pltpu.VMEM(array.shape, array.dtype) for array in operands]
        + [
            pltpu.VMEM((9, CELLS, 128), jnp.bfloat16),
            pltpu.VMEM((18 * 64, channels), jnp.bfloat16),
            pltpu.VMEM((CELLS, channels), jnp.float32),
            pltpu.VMEM((CELLS, channels), jnp.bfloat16),
            pltpu.SemaphoreType.DMA((7,)),
            pltpu.SemaphoreType.DMA((9,)),
            pltpu.SemaphoreType.DMA((9,)),
        ],
        compiler_params=pltpu.CompilerParams(collective_id=0, has_side_effects=True),
    )(*operands)


def solution(mesh):
    return jax.shard_map(
        functools.partial(on_device, mesh.shape["lon"], mesh.shape["lat"]),
        mesh=mesh,
        in_specs=(
            P("lon", "lat", None, None),
            P("lon", "lat", None),
            P("lon", "lat"),
            P(),
            P(),
            P(),
            P(),
        ),
        out_specs=P("lon", "lat", None),
        check_vma=False,
    )
```

time: 81 us -> 25.7 us (0.32)
  starting transfers between devices: 40.8 us -> 0 us
  Pallas kernels: 0 us -> 23.3 us
  matrix products: 13.4 us -> 0 us
  other arithmetic: 12.1 us -> 0 us
  waiting for transfers between devices: 5.81 us -> 0 us
  local copies, waits for them, and re-layouts: 7.26 us -> 1.57 us
    ppermute x8 -> x0, starting transfers between devices: 40.8 us -> none  [the longest x3 21.3 us: padded(): after = lax.ppermute(leading, axis, down)]
    pallas_call x0 -> x1, Pallas kernels: none -> 23.3 us  [on_device(): pl.pallas_call(functools.partial(kernel, lon_count, lat_count), out_shape...]
    dot_general x20 -> x0, matrix products: 13.4 us -> none  [the longest x18 10.2 us: grouped_filter(): total = total + jnp.dot(piece, dense, preferred_element_type=jnp.float32)]
    select_n x4 -> x0, other arithmetic: 10.8 us -> none  [the longest x1 10 us: grouped_filter(): dense = jnp.where(same_group, tiled, zero_value)]
    ppermute x8 -> x0, waiting for transfers between devices: 5.81 us -> none  [the longest x2 5.79 us: passed_along(): return lax.ppermute(value, axis, pairs)]
    another operation x3 -> x0, local copies, waits for them, and re-layouts: 3.24 us -> none  [grouped_filter(): tiled = jnp.tile(weight[first, second], (groups, 1))]
    unnamed x28 -> x1, local copies, waits for them, and re-layouts: 3.36 us -> 1.57 us
    concatenate x2 -> x0, other arithmetic: 1.29 us -> none  [padded(): array = jnp.concatenate([before, array, after], axis=dim)]
  transfers between devices with their start and end apart: 8 -> 0, of which waited for: 2 -> 0; matrix products, arithmetic and copies ran while one was open for 27% -> 0% of each run, Pallas kernels for 0% -> 0%
where the time goes in v1:
time: 25.7 us; the launch traced here: 25.6 us
  Pallas kernels  23.3 us (91%)
  local copies, waits for them, and re-layouts  1.57 us (6%)
  between operations  0.66 us (3%)
    pallas_call x1, Pallas kernels, on_device(): pl.pallas_call(functools.partial(kernel, lon_count, lat_count), out_shape...  23.3 us
    unnamed x1, local copies, waits for them, and re-layouts  1.57 us

profile of v1, /device:TPU:1, one launch (start us, length us, event | category | flops | bytes accessed | tf_op | source)
XLA Modules:
  0.0 25.6 jit_solution(14717266217166554963)
XLA Ops:
  0.7 23.3 %shard_map.73 = bf16[8,8,1024]{2,1,0:T(8,128)(2,1)} custom-call(bf16[1,1,64,1024]{3,2,1,0:T(8,128)(2,1)} %bitcast.1, s32[1,1,1024]{2,1,0:T(1,128)} %cells_hbm.1, s32[1,1]{1,0:T(1,128)S(6)} %copy.9.count_hbm, bf16[64,1024]{1,0:T(8,128)(2,1)} %enc_hbm.1, bf16[3,3,64,1024]{3,2,1,0:T(8,128)(2,1)} %near_hbm.1, bf16[3,3,64,1024]{3,2,1,0:T(8,128)(2,1)} %far_hbm.1, ...), custom_call_target="tpu_custom_call" | custom-call | tf_op jit(solution)/shard_map/pallas_call | solution.py:261
  24.0 1.6 %copy.10 = bf16[8,8,1024]{2,1,0:T(8,128)(2,1)} copy(bf16[8,8,1024]{2,1,0:T(8,128)(2,1)} %shard_map.73) | data formatting | bytes 262144

commit v2 on v1

--- a/solution.py
+++ b/solution.py
@@ -59,19 +59,16 @@
     enc_hbm,
     near_hbm,
     far_hbm,
-    mix_hbm,
-    out_ref,
+    total_ref,
+    activ_ref,
     obs_ref,
     cells_ref,
     count_ref,
     enc_ref,
     near_ref,
     far_ref,
-    mix_ref,
     slots,
     composite_ref,
-    total_ref,
-    activ_ref,
     local_sems,
     send_sems,
     recv_sems,
@@ -83,13 +80,12 @@
         (enc_hbm, enc_ref),
         (near_hbm, near_ref),
         (far_hbm, far_ref),
-        (mix_hbm, mix_ref),
     ]
     loads = [
         pltpu.make_async_copy(source, target, local_sems.at[i])
         for i, (source, target) in enumerate(pairs)
     ]
-    for load in loads:
+    for load in loads[:3]:
         load.start()
 
     lon = lax.axis_index("lon")
@@ -126,6 +122,8 @@
     loads[0].wait()
     loads[1].wait()
     loads[2].wait()
+    for load in loads[3:]:
+        load.start()
     cells = cells_ref[0]
     live = lax.broadcasted_iota(jnp.int32, cells.shape, 1) < count_ref[...]
     target = jnp.where(live, cells, -1)
@@ -138,15 +136,6 @@
     high = summed.astype(jnp.bfloat16)
     low = (summed - high.astype(jnp.float32)).astype(jnp.bfloat16)
     slots[CENTRE] = jnp.concatenate([high, low], axis=1)
-
-    lanes = lax.broadcasted_iota(jnp.int32, (64, 128), 1)
-    low_mask = jnp.where(lanes < 64, 1.0, 0.0).astype(jnp.bfloat16)
-    high_mask = jnp.where(lanes < 64, 0.0, 1.0).astype(jnp.bfloat16)
-
-    loads[3].wait()
-    loads[4].wait()
-    enc = enc_ref[...]
-    composite(enc, near_ref, composite_ref, 9, low_mask, high_mask)
 
     pl.semaphore_wait(barrier, jnp.where((lat == 0) | (lat == lat_count - 1), 5, 8))
     copies = []
@@ -167,6 +156,15 @@
     for b, copy in copies:
         with_peer(b, copy.start)
 
+    lanes = lax.broadcasted_iota(jnp.int32, (64, 128), 1)
+    low_mask = jnp.where(lanes < 64, 1.0, 0.0).astype(jnp.bfloat16)
+    high_mask = jnp.where(lanes < 64, 0.0, 1.0).astype(jnp.bfloat16)
+
+    loads[3].wait()
+    loads[4].wait()
+    enc = enc_ref[...]
+    composite(enc, near_ref, composite_ref, 9, low_mask, high_mask)
+
     loads[5].wait()
     composite(enc, far_ref, composite_ref, 0, low_mask, high_mask)
     centre = slice(CENTRE * 64, CENTRE * 64 + 64)
@@ -223,15 +221,6 @@
         total_ref[:, block] = total
         inner = 0.7978845608 * (total + 0.044715 * (total * total * total))
         activ_ref[:, block] = (0.5 * total * (1.0 + jnp.tanh(inner))).astype(jnp.bfloat16)
-
-    loads[6].wait()
-    activ = activ_ref[...]
-    for start in range(0, channels, CHUNK):
-        block = slice(start, start + CHUNK)
-        mixed = jnp.dot(activ, mix_ref[:, block], preferred_element_type=jnp.float32)
-        out_ref[:, :, block] = (
-            (total_ref[:, block] + mixed).astype(jnp.bfloat16).reshape(LON, LAT, CHUNK)
-        )
 
     for b, copy in copies:
         with_peer(b, copy.wait_send)
@@ -256,25 +245,34 @@
         enc_weight,
         near_kernel_weight,
         far_kernel_weight,
-        mix_weight,
-    )
-    return pl.pallas_call(
+    )
+    total, activ = pl.pallas_call(
         functools.partial(kernel, lon_count, lat_count),
-        out_shape=jax.ShapeDtypeStruct((LON, LAT, channels), jnp.bfloat16),
+        out_shape=[
+            jax.ShapeDtypeStruct((CELLS, channels), jnp.float32),
+            jax.ShapeDtypeStruct((CELLS, channels), jnp.bfloat16),
+        ],
         in_specs=[pl.BlockSpec(memory_space=pltpu.HBM)] * len(operands),
-        out_specs=pl.BlockSpec(memory_space=pltpu.VMEM),
+        out_specs=[pl.BlockSpec(memory_space=pltpu.VMEM)] * 2,
         scratch_shapes=[pltpu.VMEM(array.shape, array.dtype) for array in operands]
         + [
             pltpu.VMEM((9, CELLS, 128), jnp.bfloat16),
             pltpu.VMEM((18 * 64, channels), jnp.bfloat16),
-            pltpu.VMEM((CELLS, channels), jnp.float32),
-            pltpu.VMEM((CELLS, channels), jnp.bfloat16),
-            pltpu.SemaphoreType.DMA((7,)),
+            pltpu.SemaphoreType.DMA((6,)),
             pltpu.SemaphoreType.DMA((9,)),
             pltpu.SemaphoreType.DMA((9,)),
         ],
-        compiler_params=pltpu.CompilerParams(collective_id=0, has_side_effects=True),
-    )(*operands)
+        compiler_params=pltpu.CompilerParams(
+            collective_id=0, has_side_effects=True, vmem_limit_bytes=24 * 1024 * 1024
+        ),
+    )(
+        *[
+            array if array is obs_counts else pltpu.with_memory_space_constraint(array, pltpu.HBM)
+            for array in operands
+        ]
+    )
+    mixed = jnp.dot(activ, mix_weight, preferred_element_type=jnp.float32)
+    return (total + mixed).astype(jnp.bfloat16).reshape(LON, LAT, channels)
 
 
 def solution(mesh):

time: 25.7 us -> 23.2 us (0.903)
  Pallas kernels: 23.3 us -> 21.1 us
  local copies, waits for them, and re-layouts: 1.57 us -> 0.01 us
  matrix products: 0 us -> 1.14 us
    pallas_call x1, Pallas kernels: 23.3 us -> 21.1 us  [on_device(): pl.pallas_call(functools.partial(kernel, lon_count, lat_count), out_shape...]
    unnamed x1 -> x2, local copies, waits for them, and re-layouts: 1.57 us -> 0.01 us
    dot_general x0 -> x1, matrix products: none -> 1.14 us  [on_device(): mixed = jnp.dot(activ, mix_weight, preferred_element_type=jnp.float32)]
where the time goes in v2:
time: 23.2 us; the launch traced here: 23 us
  Pallas kernels  21.1 us (91%)
  matrix products  1.14 us (5%)
  between operations  0.82 us (4%)
    pallas_call x1, Pallas kernels, on_device(): pl.pallas_call(functools.partial(kernel, lon_count, lat_count), out_shape...  21.1 us
    dot_general x1, matrix products, on_device(): mixed = jnp.dot(activ, mix_weight, preferred_element_type=jnp.float32)  1.14 us

profile of v2, /device:TPU:1, one launch (start us, length us, event | category | flops | bytes accessed | tf_op | source)
XLA Modules:
  0.0 23.0 jit_solution(6792945715421841532)
XLA Ops:
  0.0 0.0 copy-start
  0.8 21.1 %shard_map.73 = (f32[64,1024]{1,0:T(8,128)S(1)}, bf16[64,1024]{1,0:T(8,128)(2,1)S(1)}) custom-call(bf16[1,1,64,1024]{3,2,1,0:T(8,128)(2,1)} %bitcast.5, s32[1,1,1024]{2,1,0:T(1,128)} %cells_hbm.1, s32[1,1]{1,0:T(1,128)S(6)} %copy.8.count_hbm, bf16[64,1024]{1,0:T(8,128)(2,1)} %enc_hbm.1, bf16[3,3,64,1024]{3,2,1,0:T(8,128)(2,1)} %near_hbm.1, ...), custom_call_target="tpu_custom_call" | custom-call | tf_op jit(solution)/shard_map/pallas_call | solution.py:249
  21.9 0.0 copy-done
  21.9 1.1 %fusion.1 = bf16[8,8,1024]{2,1,0:T(8,128)(2,1)} fusion(f32[64,1024]{1,0:T(8,128)S(1)} %get-tuple-element.7, bf16[64,1024]{1,0:T(8,128)(2,1)S(1)} %get-tuple-element.8, bf16[1024,1024]{1,0:T(8,128)(2,1)S(1)} %copy-done), kind=kOutput, calls=%fused_computation.2 | convolution fusion | flops 134348800 | bytes 2621440 | tf_op jit(solution)/shard_map/dot_general | solution.py:274
Async XLA Ops:
  0.0 21.9 %copy-start = (bf16[1024,1024]{1,0:T(8,128)(2,1)S(1)}, bf16[1024,1024]{1,0:T(8,128)(2,1)}, u32[]{:S(2)}) copy-start(bf16[1024,1024]{1,0:T(8,128)(2,1)} %param.13) | copy-start | bytes 6291460

commit v3 on v2

--- a/solution.py
+++ b/solution.py
@@ -10,6 +10,7 @@
 LON = 8
 LAT = 8
 CELLS = LON * LAT
+HALF = CELLS // 2
 MESH = pl.DeviceIdType.MESH
 OFFSETS = [(a, b) for a in (-1, 0, 1) for b in (-1, 0, 1)]
 CENTRE = 4
@@ -102,7 +103,7 @@
         else:
             pl.when(lat < lat_count - 1)(body)
 
-    remote = [(a, b) for a, b in OFFSETS if (a, b) != (0, 0)]
+    remote = [(a, b) for a in (1, -1, 0) for b in (-1, 0, 1) if (a, b) != (0, 0)]
     barrier = pltpu.get_barrier_semaphore()
     for a, b in remote:
         with_peer(
@@ -117,7 +118,7 @@
         @pl.when(lat == edge)
         def _(b=b):
             for a in (-1, 0, 1):
-                slots[slot_of(a, b)] = jnp.zeros((CELLS, 128), jnp.bfloat16)
+                slots[slot_of(a, b)] = jnp.zeros((HALF, 128), jnp.bfloat16)
 
     loads[0].wait()
     loads[1].wait()
@@ -133,9 +134,7 @@
     summed = lax.dot_general(
         onehot, obs_ref[0, 0], (((1,), (1,)), ((), ())), preferred_element_type=jnp.float32
     )
-    high = summed.astype(jnp.bfloat16)
-    low = (summed - high.astype(jnp.float32)).astype(jnp.bfloat16)
-    slots[CENTRE] = jnp.concatenate([high, low], axis=1)
+    slots[CENTRE] = jnp.concatenate([summed[:HALF], summed[HALF:]], axis=1).astype(jnp.bfloat16)
 
     pl.semaphore_wait(barrier, jnp.where((lat == 0) | (lat == lat_count - 1), 5, 8))
     copies = []
@@ -183,14 +182,18 @@
         )
         with_peer(b, arrival.wait_recv)
 
-    whole = [slots[i].astype(jnp.float32).reshape(LON, LAT, 128) for i in range(9)]
-    lon_extended = [
-        jnp.concatenate(
-            [whole[slot_of(-1, b)][LON - 1 :], whole[slot_of(0, b)], whole[slot_of(1, b)][:1]], 0
-        )
-        for b in (-1, 0, 1)
-    ]
-    row = lax.broadcasted_iota(jnp.int32, (LON + 2, LAT, 128), 1)
+    half_lon = LON // 2
+    whole = [slots[i].astype(jnp.float32).reshape(half_lon, LAT, 128) for i in range(9)]
+    left_half = lax.broadcasted_iota(jnp.int32, (1, LAT, 128), 2) < 64
+    lon_extended = []
+    for b in (-1, 0, 1):
+        minus, own, plus = [whole[slot_of(a, b)] for a in (-1, 0, 1)]
+        first = jnp.where(left_half, own[half_lon - 1 :], minus[half_lon - 1 :])
+        last = jnp.where(left_half, plus[:1], own[:1])
+        lon_extended.append(
+            jnp.concatenate([pltpu.roll(first, 64, 2), own, pltpu.roll(last, 64, 2)], 0)
+        )
+    row = lax.broadcasted_iota(jnp.int32, (half_lon + 2, LAT, 128), 1)
     before = jnp.where(
         row == 0, pltpu.roll(lon_extended[0], 1, 1), pltpu.roll(lon_extended[1], 1, 1)
     )
@@ -200,24 +203,23 @@
         pltpu.roll(lon_extended[1], LAT - 1, 1),
     )
     shifted = [before, lon_extended[1], after]
-    taps = [piece.reshape(CELLS, 128) for piece in whole]
+    taps = [piece.reshape(HALF, 128) for piece in whole]
     for a in range(3):
         for b in range(3):
-            taps.append(shifted[b][a : a + LON].reshape(CELLS, 128))
-    left_half = lax.broadcasted_iota(jnp.int32, (CELLS, 128), 1) < 64
+            taps.append(shifted[b][a : a + half_lon].reshape(HALF, 128))
+    left_half = lax.broadcasted_iota(jnp.int32, (HALF, 128), 1) < 64
     columns = []
     for i in range(0, 18, 2):
         first, second = taps[i], taps[i + 1]
-        highs = jnp.where(left_half, first, pltpu.roll(second, 64, 1))
-        lows = jnp.where(left_half, pltpu.roll(first, 64, 1), second)
-        columns.append(jnp.concatenate([highs, lows], axis=0).astype(jnp.bfloat16))
+        upper = jnp.where(left_half, first, pltpu.roll(second, 64, 1))
+        lower = jnp.where(left_half, pltpu.roll(first, 64, 1), second)
+        columns.append(jnp.concatenate([upper, lower], axis=0).astype(jnp.bfloat16))
     lhs = jnp.concatenate(columns, axis=1)
 
     channels = enc.shape[1]
     for start in range(0, channels, CHUNK):
         block = slice(start, start + CHUNK)
-        product = jnp.dot(lhs, composite_ref[:, block], preferred_element_type=jnp.float32)
-        total = product[:CELLS] + product[CELLS:]
+        total = jnp.dot(lhs, composite_ref[:, block], preferred_element_type=jnp.float32)
         total_ref[:, block] = total
         inner = 0.7978845608 * (total + 0.044715 * (total * total * total))
         activ_ref[:, block] = (0.5 * total * (1.0 + jnp.tanh(inner))).astype(jnp.bfloat16)
@@ -256,7 +258,7 @@
         out_specs=[pl.BlockSpec(memory_space=pltpu.VMEM)] * 2,
         scratch_shapes=[pltpu.VMEM(array.shape, array.dtype) for array in operands]
         + [
-            pltpu.VMEM((9, CELLS, 128), jnp.bfloat16),
+            pltpu.VMEM((9, HALF, 128), jnp.bfloat16),
             pltpu.VMEM((18 * 64, channels), jnp.bfloat16),
             pltpu.SemaphoreType.DMA((6,)),
             pltpu.SemaphoreType.DMA((9,)),

time: 23.2 us -> 23.2 us (level)
  no operation moved by 1% of the time
where the time goes in v3:
time: 23.2 us; the launch traced here: 23.1 us
  Pallas kernels  21.1 us (91%)
  matrix products  1.14 us (5%)
  between operations  0.82 us (4%)
    pallas_call x1, Pallas kernels, on_device(): pl.pallas_call(functools.partial(kernel, lon_count, lat_count), out_shape...  21.1 us
    dot_general x1, matrix products, on_device(): mixed = jnp.dot(activ, mix_weight, preferred_element_type=jnp.float32)  1.14 us

profile of v3, /device:TPU:1, one launch (start us, length us, event | category | flops | bytes accessed | tf_op | source)
XLA Modules:
  0.0 23.1 jit_solution(17836439547671674718)
XLA Ops:
  0.0 0.0 copy-start
  0.8 21.1 %shard_map.73 = (f32[64,1024]{1,0:T(8,128)S(1)}, bf16[64,1024]{1,0:T(8,128)(2,1)S(1)}) custom-call(bf16[1,1,64,1024]{3,2,1,0:T(8,128)(2,1)} %bitcast.5, s32[1,1,1024]{2,1,0:T(1,128)} %cells_hbm.1, s32[1,1]{1,0:T(1,128)S(6)} %copy.8.count_hbm, bf16[64,1024]{1,0:T(8,128)(2,1)} %enc_hbm.1, bf16[3,3,64,1024]{3,2,1,0:T(8,128)(2,1)} %near_hbm.1, ...), custom_call_target="tpu_custom_call" | custom-call | tf_op jit(solution)/shard_map/pallas_call | solution.py:251
  21.9 0.0 copy-done
  21.9 1.1 %fusion.1 = bf16[8,8,1024]{2,1,0:T(8,128)(2,1)} fusion(f32[64,1024]{1,0:T(8,128)S(1)} %get-tuple-element.7, bf16[64,1024]{1,0:T(8,128)(2,1)S(1)} %get-tuple-element.8, bf16[1024,1024]{1,0:T(8,128)(2,1)S(1)} %copy-done), kind=kOutput, calls=%fused_computation.2 | convolution fusion | flops 134348800 | bytes 2621440 | tf_op jit(solution)/shard_map/dot_general | solution.py:276
Async XLA Ops:
  0.0 21.9 %copy-start = (bf16[1024,1024]{1,0:T(8,128)(2,1)S(1)}, bf16[1024,1024]{1,0:T(8,128)(2,1)}, u32[]{:S(2)}) copy-start(bf16[1024,1024]{1,0:T(8,128)(2,1)} %param.13) | copy-start | bytes 6291460

commit v4 on v3

--- a/solution.py
+++ b/solution.py
@@ -14,6 +14,7 @@
 MESH = pl.DeviceIdType.MESH
 OFFSETS = [(a, b) for a in (-1, 0, 1) for b in (-1, 0, 1)]
 CENTRE = 4
+OBS_PARTS = 4
 CHUNK = 256
 
 
@@ -60,8 +61,10 @@
     enc_hbm,
     near_hbm,
     far_hbm,
+    mix_hbm,
     total_ref,
     activ_ref,
+    mix_ref,
     obs_ref,
     cells_ref,
     count_ref,
@@ -71,8 +74,10 @@
     slots,
     composite_ref,
     local_sems,
+    obs_sems,
     send_sems,
     recv_sems,
+    ready_sem,
 ):
     pairs = [
         (obs_hbm, obs_ref),
@@ -81,12 +86,20 @@
         (enc_hbm, enc_ref),
         (near_hbm, near_ref),
         (far_hbm, far_ref),
+        (mix_hbm, mix_ref),
     ]
     loads = [
         pltpu.make_async_copy(source, target, local_sems.at[i])
         for i, (source, target) in enumerate(pairs)
     ]
-    for load in loads[:3]:
+    features = obs_ref.shape[2] // OBS_PARTS
+    obs_loads = []
+    for i in range(OBS_PARTS):
+        part = (0, 0, slice(i * features, (i + 1) * features))
+        obs_loads.append(
+            pltpu.make_async_copy(obs_hbm.at[part], obs_ref.at[part], obs_sems.at[i])
+        )
+    for load in obs_loads + loads[1:3]:
         load.start()
 
     lon = lax.axis_index("lon")
@@ -103,15 +116,16 @@
         else:
             pl.when(lat < lat_count - 1)(body)
 
-    remote = [(a, b) for a in (1, -1, 0) for b in (-1, 0, 1) if (a, b) != (0, 0)]
+    remote = [(a, b) for a in (1, 0, -1) for b in (-1, 0, 1) if (a, b) != (0, 0)]
     barrier = pltpu.get_barrier_semaphore()
     for a, b in remote:
-        with_peer(
-            b,
-            lambda a=a, b=b: pl.semaphore_signal(
-                barrier, inc=1, device_id=peer(a, b), device_id_type=MESH
-            ),
-        )
+        if a < 1:
+            with_peer(
+                b,
+                lambda a=a, b=b: pl.semaphore_signal(
+                    barrier, inc=1, device_id=peer(a, b), device_id_type=MESH
+                ),
+            )
 
     for edge, b in ((0, -1), (lat_count - 1, 1)):
 
@@ -120,7 +134,8 @@
             for a in (-1, 0, 1):
                 slots[slot_of(a, b)] = jnp.zeros((HALF, 128), jnp.bfloat16)
 
-    loads[0].wait()
+    for load in obs_loads:
+        load.wait()
     loads[1].wait()
     loads[2].wait()
     for load in loads[3:]:
@@ -136,11 +151,13 @@
     )
     slots[CENTRE] = jnp.concatenate([summed[:HALF], summed[HALF:]], axis=1).astype(jnp.bfloat16)
 
-    pl.semaphore_wait(barrier, jnp.where((lat == 0) | (lat == lat_count - 1), 5, 8))
+    at_edge = (lat == 0) | (lat == lat_count - 1)
+    pl.semaphore_wait(barrier, jnp.where(at_edge, 3, 5))
     copies = []
     for a, b in remote:
         copies.append(
             (
+                a,
                 b,
                 pltpu.make_async_remote_copy(
                     src_ref=slots.at[CENTRE],
@@ -152,8 +169,16 @@
                 ),
             )
         )
-    for b, copy in copies:
-        with_peer(b, copy.start)
+    for a, b, copy in copies:
+        if a >= 0:
+            with_peer(b, copy.start)
+    for b in (-1, 0, 1):
+        with_peer(
+            b,
+            lambda b=b: pl.semaphore_signal(
+                ready_sem, inc=1, device_id=peer(1, b), device_id_type=MESH
+            ),
+        )
 
     lanes = lax.broadcasted_iota(jnp.int32, (64, 128), 1)
     low_mask = jnp.where(lanes < 64, 1.0, 0.0).astype(jnp.bfloat16)
@@ -170,6 +195,11 @@
     composite_ref[centre] = (
         composite_ref[centre].astype(jnp.float32) + enc.astype(jnp.float32)
     ).astype(jnp.bfloat16)
+
+    pl.semaphore_wait(ready_sem, jnp.where(at_edge, 2, 3))
+    for a, b, copy in copies:
+        if a < 0:
+            with_peer(b, copy.start)
 
     for a, b in remote:
         arrival = pltpu.make_async_remote_copy(
@@ -224,7 +254,8 @@
         inner = 0.7978845608 * (total + 0.044715 * (total * total * total))
         activ_ref[:, block] = (0.5 * total * (1.0 + jnp.tanh(inner))).astype(jnp.bfloat16)
 
-    for b, copy in copies:
+    loads[6].wait()
+    for a, b, copy in copies:
         with_peer(b, copy.wait_send)
 
 
@@ -247,22 +278,26 @@
         enc_weight,
         near_kernel_weight,
         far_kernel_weight,
-    )
-    total, activ = pl.pallas_call(
+        mix_weight,
+    )
+    total, activ, mix = pl.pallas_call(
         functools.partial(kernel, lon_count, lat_count),
         out_shape=[
             jax.ShapeDtypeStruct((CELLS, channels), jnp.float32),
             jax.ShapeDtypeStruct((CELLS, channels), jnp.bfloat16),
+            jax.ShapeDtypeStruct(mix_weight.shape, jnp.bfloat16),
         ],
         in_specs=[pl.BlockSpec(memory_space=pltpu.HBM)] * len(operands),
-        out_specs=[pl.BlockSpec(memory_space=pltpu.VMEM)] * 2,
-        scratch_shapes=[pltpu.VMEM(array.shape, array.dtype) for array in operands]
+        out_specs=[pl.BlockSpec(memory_space=pltpu.VMEM)] * 3,
+        scratch_shapes=[pltpu.VMEM(array.shape, array.dtype) for array in operands[:-1]]
         + [
             pltpu.VMEM((9, HALF, 128), jnp.bfloat16),
             pltpu.VMEM((18 * 64, channels), jnp.bfloat16),
-            pltpu.SemaphoreType.DMA((6,)),
+            pltpu.SemaphoreType.DMA((7,)),
+            pltpu.SemaphoreType.DMA((OBS_PARTS,)),
             pltpu.SemaphoreType.DMA((9,)),
             pltpu.SemaphoreType.DMA((9,)),
+            pltpu.SemaphoreType.REGULAR,
         ],
         compiler_params=pltpu.CompilerParams(
             collective_id=0, has_side_effects=True, vmem_limit_bytes=24 * 1024 * 1024
@@ -273,7 +308,7 @@
             for array in operands
         ]
     )
-    mixed = jnp.dot(activ, mix_weight, preferred_element_type=jnp.float32)
+    mixed = jnp.dot(activ, mix, preferred_element_type=jnp.float32)
     return (total + mixed).astype(jnp.bfloat16).reshape(LON, LAT, channels)
 
 

time: 23.2 us -> 21.8 us (0.940)
  Pallas kernels: 21.1 us -> 19.9 us
    pallas_call x1, Pallas kernels: 21.1 us -> 19.9 us  [on_device(): pl.pallas_call(functools.partial(kernel, lon_count, lat_count), out_shape...]
where the time goes in v4:
time: 21.8 us; the launch traced here: 21.7 us
  Pallas kernels  19.9 us (91%)
  matrix products  1.14 us (5%)
  between operations  0.66 us (3%)
    pallas_call x1, Pallas kernels, on_device(): pl.pallas_call(functools.partial(kernel, lon_count, lat_count), out_shape...  19.9 us
    dot_general x1, matrix products, on_device(): mixed = jnp.dot(activ, mix, preferred_element_type=jnp.float32)  1.14 us

profile of v4, /device:TPU:1, one launch (start us, length us, event | category | flops | bytes accessed | tf_op | source)
XLA Modules:
  0.0 21.7 jit_solution(11048191067382427481)
XLA Ops:
  0.7 19.9 %shard_map.73 = (f32[64,1024]{1,0:T(8,128)S(1)}, bf16[64,1024]{1,0:T(8,128)(2,1)S(1)}, bf16[1024,1024]{1,0:T(8,128)(2,1)S(1)}) custom-call(bf16[1,1,64,1024]{3,2,1,0:T(8,128)(2,1)} %bitcast.5, s32[1,1,1024]{2,1,0:T(1,128)} %cells_hbm.1, s32[1,1]{1,0:T(1,128)S(6)} %copy.8.count_hbm, bf16[64,1024]{1,0:T(8,128)(2,1)} %enc_hbm.1, ...), custom_call_target="tpu_custom_call" | custom-call | tf_op jit(solution)/shard_map/pallas_call | solution.py:283
  20.5 1.1 %fusion.1 = bf16[8,8,1024]{2,1,0:T(8,128)(2,1)} fusion(f32[64,1024]{1,0:T(8,128)S(1)} %get-tuple-element.8, bf16[64,1024]{1,0:T(8,128)(2,1)S(1)} %get-tuple-element.9, bf16[1024,1024]{1,0:T(8,128)(2,1)S(1)} %get-tuple-element.10), kind=kOutput, calls=%fused_computation.2 | convolution fusion | flops 134348800 | bytes 2621440 | tf_op jit(solution)/shard_map/dot_general | solution.py:311

commit v5 on v4

--- a/solution.py
+++ b/solution.py
@@ -22,7 +22,7 @@
     return (a + 1) * 3 + (b + 1)
 
 
-def composite(enc, weight_ref, composite_ref, base, low_mask, high_mask):
+def composite(enc, weight_ref, composite_ref, late, early, low_mask, high_mask):
     features, channels = enc.shape
     zero = jnp.zeros((features, 128), jnp.bfloat16)
 
@@ -43,7 +43,7 @@
             product = jnp.dot(
                 enc[:, start : start + CHUNK], blocks, preferred_element_type=jnp.float32
             )
-            row = pl.multiple_of((base + t) * features, features)
+            row = pl.multiple_of((t + jnp.where(t < 3, late, early)) * features, features)
             composite_ref[pl.ds(row, features), start : start + CHUNK] = product.astype(
                 jnp.bfloat16
             )
@@ -119,7 +119,7 @@
     remote = [(a, b) for a in (1, 0, -1) for b in (-1, 0, 1) if (a, b) != (0, 0)]
     barrier = pltpu.get_barrier_semaphore()
     for a, b in remote:
-        if a < 1:
+        if a < 0:
             with_peer(
                 b,
                 lambda a=a, b=b: pl.semaphore_signal(
@@ -138,8 +138,6 @@
         load.wait()
     loads[1].wait()
     loads[2].wait()
-    for load in loads[3:]:
-        load.start()
     cells = cells_ref[0]
     live = lax.broadcasted_iota(jnp.int32, cells.shape, 1) < count_ref[...]
     target = jnp.where(live, cells, -1)
@@ -152,7 +150,7 @@
     slots[CENTRE] = jnp.concatenate([summed[:HALF], summed[HALF:]], axis=1).astype(jnp.bfloat16)
 
     at_edge = (lat == 0) | (lat == lat_count - 1)
-    pl.semaphore_wait(barrier, jnp.where(at_edge, 3, 5))
+    pl.semaphore_wait(barrier, jnp.where(at_edge, 2, 3))
     copies = []
     for a, b in remote:
         copies.append(
@@ -170,7 +168,7 @@
             )
         )
     for a, b, copy in copies:
-        if a >= 0:
+        if a > 0:
             with_peer(b, copy.start)
     for b in (-1, 0, 1):
         with_peer(
@@ -179,6 +177,8 @@
                 ready_sem, inc=1, device_id=peer(1, b), device_id_type=MESH
             ),
         )
+    for load in loads[3:]:
+        load.start()
 
     lanes = lax.broadcasted_iota(jnp.int32, (64, 128), 1)
     low_mask = jnp.where(lanes < 64, 1.0, 0.0).astype(jnp.bfloat16)
@@ -187,69 +187,98 @@
     loads[3].wait()
     loads[4].wait()
     enc = enc_ref[...]
-    composite(enc, near_ref, composite_ref, 9, low_mask, high_mask)
+    composite(enc, near_ref, composite_ref, 3, 9, low_mask, high_mask)
 
     loads[5].wait()
-    composite(enc, far_ref, composite_ref, 0, low_mask, high_mask)
-    centre = slice(CENTRE * 64, CENTRE * 64 + 64)
+    composite(enc, far_ref, composite_ref, 0, 3, low_mask, high_mask)
+    centre = slice((CENTRE + 3) * 64, (CENTRE + 4) * 64)
     composite_ref[centre] = (
         composite_ref[centre].astype(jnp.float32) + enc.astype(jnp.float32)
     ).astype(jnp.bfloat16)
 
     pl.semaphore_wait(ready_sem, jnp.where(at_edge, 2, 3))
     for a, b, copy in copies:
-        if a < 0:
+        if a < 1:
             with_peer(b, copy.start)
 
-    for a, b in remote:
-        arrival = pltpu.make_async_remote_copy(
-            src_ref=slots.at[CENTRE],
-            dst_ref=slots.at[slot_of(a, b)],
-            send_sem=send_sems.at[slot_of(a, b)],
-            recv_sem=recv_sems.at[slot_of(a, b)],
-            device_id=peer(a, b),
-            device_id_type=MESH,
-        )
-        with_peer(b, arrival.wait_recv)
+    def await_from(a):
+        for c, b in remote:
+            if c == a:
+                arrival = pltpu.make_async_remote_copy(
+                    src_ref=slots.at[CENTRE],
+                    dst_ref=slots.at[slot_of(a, b)],
+                    send_sem=send_sems.at[slot_of(a, b)],
+                    recv_sem=recv_sems.at[slot_of(a, b)],
+                    device_id=peer(a, b),
+                    device_id_type=MESH,
+                )
+                with_peer(b, arrival.wait_recv)
 
     half_lon = LON // 2
-    whole = [slots[i].astype(jnp.float32).reshape(half_lon, LAT, 128) for i in range(9)]
-    left_half = lax.broadcasted_iota(jnp.int32, (1, LAT, 128), 2) < 64
-    lon_extended = []
-    for b in (-1, 0, 1):
-        minus, own, plus = [whole[slot_of(a, b)] for a in (-1, 0, 1)]
-        first = jnp.where(left_half, own[half_lon - 1 :], minus[half_lon - 1 :])
-        last = jnp.where(left_half, plus[:1], own[:1])
-        lon_extended.append(
-            jnp.concatenate([pltpu.roll(first, 64, 2), own, pltpu.roll(last, 64, 2)], 0)
-        )
-    row = lax.broadcasted_iota(jnp.int32, (half_lon + 2, LAT, 128), 1)
-    before = jnp.where(
-        row == 0, pltpu.roll(lon_extended[0], 1, 1), pltpu.roll(lon_extended[1], 1, 1)
-    )
-    after = jnp.where(
-        row == LAT - 1,
-        pltpu.roll(lon_extended[2], LAT - 1, 1),
-        pltpu.roll(lon_extended[1], LAT - 1, 1),
-    )
-    shifted = [before, lon_extended[1], after]
-    taps = [piece.reshape(HALF, 128) for piece in whole]
-    for a in range(3):
-        for b in range(3):
-            taps.append(shifted[b][a : a + half_lon].reshape(HALF, 128))
-    left_half = lax.broadcasted_iota(jnp.int32, (HALF, 128), 1) < 64
-    columns = []
-    for i in range(0, 18, 2):
-        first, second = taps[i], taps[i + 1]
-        upper = jnp.where(left_half, first, pltpu.roll(second, 64, 1))
-        lower = jnp.where(left_half, pltpu.roll(first, 64, 1), second)
-        columns.append(jnp.concatenate([upper, lower], axis=0).astype(jnp.bfloat16))
-    lhs = jnp.concatenate(columns, axis=1)
+
+    def blocks_of(a):
+        return [
+            slots[slot_of(a, b)].astype(jnp.float32).reshape(half_lon, LAT, 128)
+            for b in (-1, 0, 1)
+        ]
+
+    left = lax.broadcasted_iota(jnp.int32, (1, LAT, 128), 2) < 64
+
+    def lat_shifted(rows_of):
+        row = lax.broadcasted_iota(jnp.int32, rows_of[0].shape, 1)
+        before = jnp.where(row == 0, pltpu.roll(rows_of[0], 1, 1), pltpu.roll(rows_of[1], 1, 1))
+        after = jnp.where(
+            row == LAT - 1,
+            pltpu.roll(rows_of[2], LAT - 1, 1),
+            pltpu.roll(rows_of[1], LAT - 1, 1),
+        )
+        return [before, rows_of[1], after]
+
+    def stacked(taps):
+        taps = [tap.reshape(HALF, 128) for tap in taps]
+        left_half = lax.broadcasted_iota(jnp.int32, (HALF, 128), 1) < 64
+        columns = []
+        for first, second in zip(taps[::2], taps[1::2]):
+            upper = jnp.where(left_half, first, pltpu.roll(second, 64, 1))
+            lower = jnp.where(left_half, pltpu.roll(first, 64, 1), second)
+            columns.append(jnp.concatenate([upper, lower], axis=0).astype(jnp.bfloat16))
+        return jnp.concatenate(columns, axis=1)
 
     channels = enc.shape[1]
+    late_rows = 6 * 64
+
+    await_from(0)
+    await_from(1)
+    own, plus = blocks_of(0), blocks_of(1)
+    ahead = [
+        jnp.concatenate([own[b], pltpu.roll(jnp.where(left, plus[b][:1], own[b][:1]), 64, 2)], 0)
+        for b in range(3)
+    ]
+    ahead = lat_shifted(ahead)
+    early = stacked(
+        own
+        + plus
+        + [piece[:half_lon] for piece in ahead]
+        + [piece[1 : 1 + half_lon] for piece in ahead]
+    )
     for start in range(0, channels, CHUNK):
         block = slice(start, start + CHUNK)
-        total = jnp.dot(lhs, composite_ref[:, block], preferred_element_type=jnp.float32)
+        total_ref[:, block] = jnp.dot(
+            early, composite_ref[late_rows:, block], preferred_element_type=jnp.float32
+        )
+
+    await_from(-1)
+    own, minus = blocks_of(0), blocks_of(-1)
+    behind = []
+    for b in range(3):
+        first = jnp.where(left, own[b][half_lon - 1 :], minus[b][half_lon - 1 :])
+        behind.append(jnp.concatenate([pltpu.roll(first, 64, 2), own[b][: half_lon - 1]], 0))
+    late = stacked(minus + lat_shifted(behind))
+    for start in range(0, channels, CHUNK):
+        block = slice(start, start + CHUNK)
+        total = total_ref[:, block] + jnp.dot(
+            late, composite_ref[:late_rows, block], preferred_element_type=jnp.float32
+        )
         total_ref[:, block] = total
         inner = 0.7978845608 * (total + 0.044715 * (total * total * total))
         activ_ref[:, block] = (0.5 * total * (1.0 + jnp.tanh(inner))).astype(jnp.bfloat16)

time: 21.8 us -> 22.2 us (1.018)
  Pallas kernels: 19.9 us -> 20.2 us
    pallas_call x1, Pallas kernels: 19.9 us -> 20.2 us  [on_device(): pl.pallas_call(functools.partial(kernel, lon_count, lat_count), out_shape...]
where the time goes in v5:
time: 22.2 us; the launch traced here: 22.1 us
  Pallas kernels  20.2 us (91%)
  matrix products  1.14 us (5%)
  between operations  0.66 us (3%)
    pallas_call x1, Pallas kernels, on_device(): pl.pallas_call(functools.partial(kernel, lon_count, lat_count), out_shape...  20.2 us
    dot_general x1, matrix products, on_device(): mixed = jnp.dot(activ, mix, preferred_element_type=jnp.float32)  1.14 us

profile of v5, /device:TPU:1, one launch (start us, length us, event | category | flops | bytes accessed | tf_op | source)
XLA Modules:
  0.0 22.1 jit_solution(17712391968181723069)
XLA Ops:
  0.7 20.2 %shard_map.73 = (f32[64,1024]{1,0:T(8,128)S(1)}, bf16[64,1024]{1,0:T(8,128)(2,1)S(1)}, bf16[1024,1024]{1,0:T(8,128)(2,1)S(1)}) custom-call(bf16[1,1,64,1024]{3,2,1,0:T(8,128)(2,1)} %bitcast.5, s32[1,1,1024]{2,1,0:T(1,128)} %cells_hbm.1, s32[1,1]{1,0:T(1,128)S(6)} %copy.8.count_hbm, bf16[64,1024]{1,0:T(8,128)(2,1)} %enc_hbm.1, ...), custom_call_target="tpu_custom_call" | custom-call | tf_op jit(solution)/shard_map/pallas_call | solution.py:312
  20.9 1.1 %fusion.1 = bf16[8,8,1024]{2,1,0:T(8,128)(2,1)} fusion(f32[64,1024]{1,0:T(8,128)S(1)} %get-tuple-element.8, bf16[64,1024]{1,0:T(8,128)(2,1)S(1)} %get-tuple-element.9, bf16[1024,1024]{1,0:T(8,128)(2,1)S(1)} %get-tuple-element.10), kind=kOutput, calls=%fused_computation.2 | convolution fusion | flops 134348800 | bytes 2621440 | tf_op jit(solution)/shard_map/dot_general | solution.py:340

commit v6 on v5

--- a/solution.py
+++ b/solution.py
@@ -99,7 +99,7 @@
         obs_loads.append(
             pltpu.make_async_copy(obs_hbm.at[part], obs_ref.at[part], obs_sems.at[i])
         )
-    for load in obs_loads + loads[1:3]:
+    for load in loads[1:3] + obs_loads:
         load.start()
 
     lon = lax.axis_index("lon")
@@ -119,7 +119,7 @@
     remote = [(a, b) for a in (1, 0, -1) for b in (-1, 0, 1) if (a, b) != (0, 0)]
     barrier = pltpu.get_barrier_semaphore()
     for a, b in remote:
-        if a < 0:
+        if a < 1:
             with_peer(
                 b,
                 lambda a=a, b=b: pl.semaphore_signal(
@@ -134,8 +134,6 @@
             for a in (-1, 0, 1):
                 slots[slot_of(a, b)] = jnp.zeros((HALF, 128), jnp.bfloat16)
 
-    for load in obs_loads:
-        load.wait()
     loads[1].wait()
     loads[2].wait()
     cells = cells_ref[0]
@@ -144,13 +142,15 @@
     onehot = jnp.where(
         lax.broadcasted_iota(jnp.int32, (CELLS, cells.shape[1]), 0) == target, 1.0, 0.0
     ).astype(jnp.bfloat16)
+    for load in obs_loads:
+        load.wait()
     summed = lax.dot_general(
         onehot, obs_ref[0, 0], (((1,), (1,)), ((), ())), preferred_element_type=jnp.float32
     )
     slots[CENTRE] = jnp.concatenate([summed[:HALF], summed[HALF:]], axis=1).astype(jnp.bfloat16)
 
     at_edge = (lat == 0) | (lat == lat_count - 1)
-    pl.semaphore_wait(barrier, jnp.where(at_edge, 2, 3))
+    pl.semaphore_wait(barrier, jnp.where(at_edge, 3, 5))
     copies = []
     for a, b in remote:
         copies.append(
@@ -168,7 +168,7 @@
             )
         )
     for a, b, copy in copies:
-        if a > 0:
+        if a >= 0:
             with_peer(b, copy.start)
     for b in (-1, 0, 1):
         with_peer(
@@ -198,7 +198,7 @@
 
     pl.semaphore_wait(ready_sem, jnp.where(at_edge, 2, 3))
     for a, b, copy in copies:
-        if a < 1:
+        if a < 0:
             with_peer(b, copy.start)
 
     def await_from(a):

time: 22.2 us -> 21.6 us (0.973)
  Pallas kernels: 20.2 us -> 19.6 us
    pallas_call x1, Pallas kernels: 20.2 us -> 19.6 us  [on_device(): pl.pallas_call(functools.partial(kernel, lon_count, lat_count), out_shape...]
where the time goes in v6:
time: 21.6 us; the launch traced here: 21.4 us
  Pallas kernels  19.6 us (91%)
  matrix products  1.14 us (5%)
  between operations  0.66 us (3%)
    pallas_call x1, Pallas kernels, on_device(): pl.pallas_call(functools.partial(kernel, lon_count, lat_count), out_shape...  19.6 us
    dot_general x1, matrix products, on_device(): mixed = jnp.dot(activ, mix, preferred_element_type=jnp.float32)  1.14 us

profile of v6, /device:TPU:1, one launch (start us, length us, event | category | flops | bytes accessed | tf_op | source)
XLA Modules:
  0.0 21.4 jit_solution(8956476297855699464)
XLA Ops:
  0.7 19.6 %shard_map.73 = (f32[64,1024]{1,0:T(8,128)S(1)}, bf16[64,1024]{1,0:T(8,128)(2,1)S(1)}, bf16[1024,1024]{1,0:T(8,128)(2,1)S(1)}) custom-call(bf16[1,1,64,1024]{3,2,1,0:T(8,128)(2,1)} %bitcast.5, s32[1,1,1024]{2,1,0:T(1,128)} %cells_hbm.1, s32[1,1]{1,0:T(1,128)S(6)} %copy.8.count_hbm, bf16[64,1024]{1,0:T(8,128)(2,1)} %enc_hbm.1, ...), custom_call_target="tpu_custom_call" | custom-call | tf_op jit(solution)/shard_map/pallas_call | solution.py:312
  20.2 1.1 %fusion.1 = bf16[8,8,1024]{2,1,0:T(8,128)(2,1)} fusion(f32[64,1024]{1,0:T(8,128)S(1)} %get-tuple-element.8, bf16[64,1024]{1,0:T(8,128)(2,1)S(1)} %get-tuple-element.9, bf16[1024,1024]{1,0:T(8,128)(2,1)S(1)} %get-tuple-element.10), kind=kOutput, calls=%fused_computation.2 | convolution fusion | flops 134348800 | bytes 2621440 | tf_op jit(solution)/shard_map/dot_general | solution.py:340

commit v7 on v6

--- a/solution.py
+++ b/solution.py
@@ -62,15 +62,16 @@
     near_hbm,
     far_hbm,
     mix_hbm,
-    total_ref,
-    activ_ref,
-    mix_ref,
+    out_ref,
     obs_ref,
     cells_ref,
     count_ref,
     enc_ref,
     near_ref,
     far_ref,
+    mix_ref,
+    total_ref,
+    activ_ref,
     slots,
     composite_ref,
     local_sems,
@@ -284,6 +285,12 @@
         activ_ref[:, block] = (0.5 * total * (1.0 + jnp.tanh(inner))).astype(jnp.bfloat16)
 
     loads[6].wait()
+    for start in range(0, channels, CHUNK):
+        block = slice(start, start + CHUNK)
+        mixed = jnp.dot(activ_ref[...], mix_ref[:, block], preferred_element_type=jnp.float32)
+        out_ref[:, :, block] = (
+            (total_ref[:, block] + mixed).astype(jnp.bfloat16).reshape(LON, LAT, CHUNK)
+        )
     for a, b, copy in copies:
         with_peer(b, copy.wait_send)
 
@@ -309,17 +316,15 @@
         far_kernel_weight,
         mix_weight,
     )
-    total, activ, mix = pl.pallas_call(
+    return pl.pallas_call(
         functools.partial(kernel, lon_count, lat_count),
-        out_shape=[
-            jax.ShapeDtypeStruct((CELLS, channels), jnp.float32),
-            jax.ShapeDtypeStruct((CELLS, channels), jnp.bfloat16),
-            jax.ShapeDtypeStruct(mix_weight.shape, jnp.bfloat16),
-        ],
+        out_shape=jax.ShapeDtypeStruct((LON, LAT, channels), jnp.bfloat16),
         in_specs=[pl.BlockSpec(memory_space=pltpu.HBM)] * len(operands),
-        out_specs=[pl.BlockSpec(memory_space=pltpu.VMEM)] * 3,
-        scratch_shapes=[pltpu.VMEM(array.shape, array.dtype) for array in operands[:-1]]
+        out_specs=pl.BlockSpec(memory_space=pltpu.VMEM),
+        scratch_shapes=[pltpu.VMEM(array.shape, array.dtype) for array in operands]
         + [
+            pltpu.VMEM((CELLS, channels), jnp.float32),
+            pltpu.VMEM((CELLS, channels), jnp.bfloat16),
             pltpu.VMEM((9, HALF, 128), jnp.bfloat16),
             pltpu.VMEM((18 * 64, channels), jnp.bfloat16),
             pltpu.SemaphoreType.DMA((7,)),
@@ -337,8 +342,6 @@
             for array in operands
         ]
     )
-    mixed = jnp.dot(activ, mix, preferred_element_type=jnp.float32)
-    return (total + mixed).astype(jnp.bfloat16).reshape(LON, LAT, channels)
 
 
 def solution(mesh):

time: 21.6 us -> 21.6 us (level)
  matrix products: 1.14 us -> 0 us
  local copies, waits for them, and re-layouts: 0 us -> 0.66 us
  Pallas kernels: 19.6 us -> 20.1 us
    dot_general x1 -> x0, matrix products: 1.14 us -> none  [on_device(): mixed = jnp.dot(activ, mix, preferred_element_type=jnp.float32)]
    unnamed x0 -> x1, local copies, waits for them, and re-layouts: none -> 0.66 us
    pallas_call x1, Pallas kernels: 19.6 us -> 20.1 us  [on_device(): pl.pallas_call(functools.partial(kernel, lon_count, lat_count), out_shape...]
where the time goes in v7:
time: 21.6 us; the launch traced here: 21.4 us
  Pallas kernels  20.1 us (93%)
  local copies, waits for them, and re-layouts  0.66 us (3%)
  between operations  0.66 us (3%)
    pallas_call x1, Pallas kernels, on_device(): pl.pallas_call(functools.partial(kernel, lon_count, lat_count), out_shape...  20.1 us
    unnamed x1, local copies, waits for them, and re-layouts  0.66 us

profile of v7, /device:TPU:1, one launch (start us, length us, event | category | flops | bytes accessed | tf_op | source)
XLA Modules:
  0.0 21.4 jit_solution(3843197929199742197)
XLA Ops:
  0.7 20.1 %shard_map.73 = bf16[8,8,1024]{2,1,0:T(8,128)(2,1)S(1)} custom-call(bf16[1,1,64,1024]{3,2,1,0:T(8,128)(2,1)} %bitcast.1, s32[1,1,1024]{2,1,0:T(1,128)} %cells_hbm.1, s32[1,1]{1,0:T(1,128)S(6)} %copy.9.count_hbm, bf16[64,1024]{1,0:T(8,128)(2,1)} %enc_hbm.1, bf16[3,3,64,1024]{3,2,1,0:T(8,128)(2,1)} %near_hbm.1, bf16[3,3,64,1024]{3,2,1,0:T(8,128)(2,1)} %far_hbm.1, ...), custom_call_target="tpu_custom_call" | custom-call | tf_op jit(solution)/shard_map/pallas_call | solution.py:319
  20.7 0.7 %copy.10 = bf16[8,8,1024]{2,1,0:T(8,128)(2,1)} copy(bf16[8,8,1024]{2,1,0:T(8,128)(2,1)S(1)} %shard_map.73) | data formatting | bytes 262144

commit v8 on v7

--- a/solution.py
+++ b/solution.py
@@ -71,7 +71,6 @@
     far_ref,
     mix_ref,
     total_ref,
-    activ_ref,
     slots,
     composite_ref,
     local_sems,
@@ -268,6 +267,7 @@
             early, composite_ref[late_rows:, block], preferred_element_type=jnp.float32
         )
 
+    loads[6].wait()
     await_from(-1)
     own, minus = blocks_of(0), blocks_of(-1)
     behind = []
@@ -275,6 +275,7 @@
         first = jnp.where(left, own[b][half_lon - 1 :], minus[b][half_lon - 1 :])
         behind.append(jnp.concatenate([pltpu.roll(first, 64, 2), own[b][: half_lon - 1]], 0))
     late = stacked(minus + lat_shifted(behind))
+    activs = []
     for start in range(0, channels, CHUNK):
         block = slice(start, start + CHUNK)
         total = total_ref[:, block] + jnp.dot(
@@ -282,12 +283,12 @@
         )
         total_ref[:, block] = total
         inner = 0.7978845608 * (total + 0.044715 * (total * total * total))
-        activ_ref[:, block] = (0.5 * total * (1.0 + jnp.tanh(inner))).astype(jnp.bfloat16)
-
-    loads[6].wait()
+        activs.append((0.5 * total * (1.0 + jnp.tanh(inner))).astype(jnp.bfloat16))
+
+    activ = jnp.concatenate(activs, axis=1)
     for start in range(0, channels, CHUNK):
         block = slice(start, start + CHUNK)
-        mixed = jnp.dot(activ_ref[...], mix_ref[:, block], preferred_element_type=jnp.float32)
+        mixed = jnp.dot(activ, mix_ref[:, block], preferred_element_type=jnp.float32)
         out_ref[:, :, block] = (
             (total_ref[:, block] + mixed).astype(jnp.bfloat16).reshape(LON, LAT, CHUNK)
         )
@@ -324,7 +325,6 @@
         scratch_shapes=[pltpu.VMEM(array.shape, array.dtype) for array in operands]
         + [
             pltpu.VMEM((CELLS, channels), jnp.float32),
-            pltpu.VMEM((CELLS, channels), jnp.bfloat16),
             pltpu.VMEM((9, HALF, 128), jnp.bfloat16),
             pltpu.VMEM((18 * 64, channels), jnp.bfloat16),
             pltpu.SemaphoreType.DMA((7,)),

time: 21.6 us -> 21.5 us (level)
  no operation moved by 1% of the time
where the time goes in v8:
time: 21.5 us; the launch traced here: 21.3 us
  Pallas kernels  20 us (93%)
  local copies, waits for them, and re-layouts  0.66 us (3%)
  between operations  0.66 us (3%)
    pallas_call x1, Pallas kernels, on_device(): pl.pallas_call(functools.partial(kernel, lon_count, lat_count), out_shape...  20 us
    unnamed x1, local copies, waits for them, and re-layouts  0.66 us

profile of v8, /device:TPU:1, one launch (start us, length us, event | category | flops | bytes accessed | tf_op | source)
XLA Modules:
  0.0 21.3 jit_solution(10833520679727044940)
XLA Ops:
  0.7 20.0 %shard_map.73 = bf16[8,8,1024]{2,1,0:T(8,128)(2,1)S(1)} custom-call(bf16[1,1,64,1024]{3,2,1,0:T(8,128)(2,1)} %bitcast.1, s32[1,1,1024]{2,1,0:T(1,128)} %cells_hbm.1, s32[1,1]{1,0:T(1,128)S(6)} %copy.9.count_hbm, bf16[64,1024]{1,0:T(8,128)(2,1)} %enc_hbm.1, bf16[3,3,64,1024]{3,2,1,0:T(8,128)(2,1)} %near_hbm.1, bf16[3,3,64,1024]{3,2,1,0:T(8,128)(2,1)} %far_hbm.1, ...), custom_call_target="tpu_custom_call" | custom-call | tf_op jit(solution)/shard_map/pallas_call | solution.py:320
  20.6 0.7 %copy.10 = bf16[8,8,1024]{2,1,0:T(8,128)(2,1)} copy(bf16[8,8,1024]{2,1,0:T(8,128)(2,1)S(1)} %shard_map.73) | data formatting | bytes 262144

commit v9 on v8

--- a/solution.py
+++ b/solution.py
@@ -14,7 +14,7 @@
 MESH = pl.DeviceIdType.MESH
 OFFSETS = [(a, b) for a in (-1, 0, 1) for b in (-1, 0, 1)]
 CENTRE = 4
-OBS_PARTS = 4
+OBS_PARTS = 8
 CHUNK = 256
 
 

time: 21.5 us -> 21.6 us (level)
  no operation moved by 1% of the time
where the time goes in v9:
time: 21.6 us; the launch traced here: 21.3 us
  Pallas kernels  20 us (93%)
  local copies, waits for them, and re-layouts  0.66 us (3%)
  between operations  0.66 us (3%)
    pallas_call x1, Pallas kernels, on_device(): pl.pallas_call(functools.partial(kernel, lon_count, lat_count), out_shape...  20 us
    unnamed x1, local copies, waits for them, and re-layouts  0.66 us

profile of v9, /device:TPU:1, one launch (start us, length us, event | category | flops | bytes accessed | tf_op | source)
XLA Modules:
  0.0 21.3 jit_solution(13197419921789997776)
XLA Ops:
  0.7 20.0 %shard_map.73 = bf16[8,8,1024]{2,1,0:T(8,128)(2,1)S(1)} custom-call(bf16[1,1,64,1024]{3,2,1,0:T(8,128)(2,1)} %bitcast.1, s32[1,1,1024]{2,1,0:T(1,128)} %cells_hbm.1, s32[1,1]{1,0:T(1,128)S(6)} %copy.9.count_hbm, bf16[64,1024]{1,0:T(8,128)(2,1)} %enc_hbm.1, bf16[3,3,64,1024]{3,2,1,0:T(8,128)(2,1)} %near_hbm.1, bf16[3,3,64,1024]{3,2,1,0:T(8,128)(2,1)} %far_hbm.1, ...), custom_call_target="tpu_custom_call" | custom-call | tf_op jit(solution)/shard_map/pallas_call | solution.py:320
  20.7 0.7 %copy.10 = bf16[8,8,1024]{2,1,0:T(8,128)(2,1)} copy(bf16[8,8,1024]{2,1,0:T(8,128)(2,1)S(1)} %shard_map.73) | data formatting | bytes 262144
